TPU v7x, 256 devices: a whole 4x4x8 slice. The times are simulated.
256 devices in a mesh: blk: 16 (over y, x_hi, core), uly: 16 (over z, x_lo).
Axes of the slice: x: 4 (x_hi: 2, x_lo: 2; x = x_hi * 2 + x_lo), y: 4, z: 8, core: 2. Of those that a mesh axis runs over, the one named last changes fastest.
Arguments:
- queries: bfloat16 [65536, 4096], P(('blk', 'uly')), may hold values from -6 to 6
- keys: bfloat16 [65536, 4096], P(('blk', 'uly')), may hold values from -6 to 6
- values: bfloat16 [65536, 4096], P(('blk', 'uly')), may hold values from -6 to 6
- doc_start: int32 [65536], P('blk'), may hold values from 0 to 65535, as said below
Outputs:
- attended: bfloat16 [65536, 4096], P(('blk', 'uly'))
Inputs may be any that keep to these rules, and one draw needn't show every extreme that they name: doc_start[0] = 0, and for t > 0 doc_start[t] is either t or doc_start[t - 1].
All inputs are finite; a program needn't handle non-finite values.
Results may differ from a plain program's by a relative error of at most 0.0026.
Values may be sent and summed in bfloat16 or wider, within the bound.
A program may use at most 128 MiB of HBM per device.

v0:
```python
import math

import jax
import jax.numpy as jnp
from jax import lax
from jax.sharding import PartitionSpec as P

HEAD_DIM = 128


def shifted(block, axis, distance):
    devices = range(lax.axis_size(axis))
    route = [(i - distance, i) for i in devices if i - distance in devices]
    return lax.ppermute(block, axis, route)


def previous_rows(key_stretch, value_stretch, window):
    key_prior, value_prior = shifted((key_stretch, value_stretch), "blk", 1)
    return (key_prior[-window:], value_prior[-window:])


def shards(queries, keys, values, doc_start):
    stretch_len = doc_start.shape[0]
    window = stretch_len // 2
    qblock = min(512, stretch_len)
    query_stretch, key_stretch, value_stretch = (
        lax.all_to_all(queries, "uly", split_axis=1, concat_axis=0, tiled=True),
        lax.all_to_all(keys, "uly", split_axis=1, concat_axis=0, tiled=True),
        lax.all_to_all(values, "uly", split_axis=1, concat_axis=0, tiled=True),
    )
    key_prior, value_prior = previous_rows(key_stretch, value_stretch, window)
    group_width = query_stretch.shape[1]
    group_heads = group_width // HEAD_DIM
    query_all = query_stretch.reshape(stretch_len, group_heads, HEAD_DIM)
    keys_wide = jnp.concatenate([key_prior, key_stretch], axis=0).reshape(
        stretch_len + window, group_heads, HEAD_DIM
    )
    values_wide = jnp.concatenate([value_prior, value_stretch], axis=0).reshape(
        stretch_len + window, group_heads, HEAD_DIM
    )
    anchor = lax.axis_index("blk") * stretch_len
    score_scale = 1.0 / math.sqrt(HEAD_DIM)

    def attend_span(first, query_rows, starts, skipped):
        span_len = qblock + window - skipped
        key_rows = lax.dynamic_slice_in_dim(keys_wide, first + skipped, span_len, 0)
        value_rows = lax.dynamic_slice_in_dim(values_wide, first + skipped, span_len, 0)
        query_pos = anchor + first + jnp.arange(qblock, dtype=jnp.int32)
        key_pos = anchor + first - window + skipped + jnp.arange(span_len, dtype=jnp.int32)
        allowed = (
            (key_pos[None, :] <= query_pos[:, None])
            & (key_pos[None, :] > query_pos[:, None] - window)
            & (key_pos[None, :] >= starts[:, None])
        )
        scores = (
            jnp.einsum("qhd,khd->hqk", query_rows, key_rows, preferred_element_type=jnp.float32)
            * score_scale
        )
        scores = jnp.where(allowed[None], scores, -jnp.inf)
        row_max = jnp.max(scores, axis=-1, keepdims=True)
        probs = jnp.exp(scores - row_max)
        totals = jnp.sum(probs, axis=-1)
        weights = probs.astype(jnp.bfloat16)
        mixed = jnp.einsum("hqk,khd->qhd", weights, value_rows, preferred_element_type=jnp.float32)
        mixed = mixed / jnp.transpose(totals)[:, :, None]
        return mixed.astype(jnp.bfloat16).reshape(qblock, group_width)

    def attend_block(block_index):
        first = block_index * qblock
        query_rows = lax.dynamic_slice_in_dim(query_all, first, qblock, 0)
        starts = lax.dynamic_slice_in_dim(doc_start, first, qblock, 0)
        return attend_span(first, query_rows, starts, 0)

    blocks = lax.map(attend_block, jnp.arange(stretch_len // qblock, dtype=jnp.int32))
    result = blocks.reshape(stretch_len, group_width)
    return lax.all_to_all(result, "uly", split_axis=0, concat_axis=1, tiled=True)


def solution(mesh):
    return jax.shard_map(
        shards,
        mesh=mesh,
        in_specs=(
            P(("blk", "uly"), None),
            P(("blk", "uly"), None),
            P(("blk", "uly"), None),
            P("blk"),
        ),
        out_specs=P(("blk", "uly"), None),
        check_vma=False,
    )
```

profile of v0, /device:TPU:12, one launch (start us, length us, event | category | flops | bytes accessed | tf_op | source)
XLA Modules:
  0.0 401.5 jit_solution(1465605567269902277)
XLA Ops:
  0.0 4.1 %copy.42 = bf16[256,4096]{0,1:T(8,128)(2,1)} copy(bf16[256,4096]{1,0:T(8,128)(2,1)} %param.7) | data formatting | bytes 4194304 | tf_op args[1]
  4.1 9.2 %all-to-all-start.2 = ((bf16[256,16,256]{0,2,1:T(8,128)(2,1)}), bf16[256,16,256]{0,2,1:T(8,128)(2,1)S(1)}, u32[]{:S(2)}, u32[]{:S(2)}) async-start(bf16[256,16,256]{0,2,1:T(8,128)(2,1)} %bitcast.42), calls=%async_computation.2 | async-start | bytes 4194304 | tf_op jit(solution)/shard_map/all_to_all | solution.py:28
  13.3 4.1 %copy.36 = bf16[256,4096]{0,1:T(8,128)(2,1)} copy(bf16[256,4096]{1,0:T(8,128)(2,1)} %param.8) | data formatting | bytes 4194304 | tf_op args[2]
  17.4 46.5 %all-to-all-done.2 = bf16[256,16,256]{0,2,1:T(8,128)(2,1)S(1)} async-done(((bf16[256,16,256]{0,2,1:T(8,128)(2,1)}), bf16[256,16,256]{0,2,1:T(8,128)(2,1)S(1)}, u32[]{:S(2)}, u32[]{:S(2)}) %all-to-all-start.2) | async-done | bytes 2097184 | tf_op jit(solution)/shard_map/all_to_all | solution.py:28
  63.8 4.4 %all-to-all-start = ((bf16[256,16,256]{0,2,1:T(8,128)(2,1)}), bf16[256,16,256]{0,2,1:T(8,128)(2,1)}, u32[]{:S(2)}, u32[]{:S(2)}) async-start(bf16[256,16,256]{0,2,1:T(8,128)(2,1)} %bitcast.41), calls=%async_computation | async-start | bytes 4194304 | tf_op jit(solution)/shard_map/all_to_all | solution.py:29
  68.3 4.1 %copy.40 = bf16[256,4096]{0,1:T(8,128)(2,1)} copy(bf16[256,4096]{1,0:T(8,128)(2,1)} %param.6) | data formatting | bytes 4194304 | tf_op args[0]
  72.4 45.6 %all-to-all-done = bf16[256,16,256]{0,2,1:T(8,128)(2,1)} async-done(((bf16[256,16,256]{0,2,1:T(8,128)(2,1)}), bf16[256,16,256]{0,2,1:T(8,128)(2,1)}, u32[]{:S(2)}, u32[]{:S(2)}) %all-to-all-start) | async-done | bytes 2097184 | tf_op jit(solution)/shard_map/all_to_all | solution.py:29
  118.0 4.4 %all-to-all-start.1 = ((bf16[256,16,256]{0,2,1:T(8,128)(2,1)}), bf16[256,16,256]{0,2,1:T(8,128)(2,1)}, u32[]{:S(2)}, u32[]{:S(2)}) async-start(bf16[256,16,256]{0,2,1:T(8,128)(2,1)} %bitcast.40), calls=%async_computation.1 | async-start | bytes 4194304 | tf_op jit(solution)/shard_map/all_to_all | solution.py:27
  122.5 2.4 copy.43
  124.8 1.9 collective-permute-start.1
  126.7 3.9 copy.37
  130.7 3.8 collective-permute-start
  134.5 2.5 copy.45
  137.0 4.1 %copy.38 = bf16[16,256,256]{1,0,2:T(8,128)(2,1)} copy(bf16[16,256,256]{1,2,0:T(8,128)(2,1)} %bitcast.8) | data formatting | bytes 4194304 | tf_op jit(solution)/shard_map/all_to_all | solution.py:29
  141.1 4.3 %concatenate.17 = bf16[4096,2,128]{0,2,1:T(8,128)(2,1)} reshape(bf16[16,256,256]{1,0,2:T(8,128)(2,1)} %copy.38) | data formatting | bytes 4194304 | tf_op jit(solution)/shard_map/concatenate | solution.py:38
  145.4 2.4 concatenate.20
  147.8 24.5 %all-to-all-done.1 = bf16[256,16,256]{0,2,1:T(8,128)(2,1)} async-done(((bf16[256,16,256]{0,2,1:T(8,128)(2,1)}), bf16[256,16,256]{0,2,1:T(8,128)(2,1)}, u32[]{:S(2)}, u32[]{:S(2)}) %all-to-all-start.1) | async-done | bytes 2097184 | tf_op jit(solution)/shard_map/all_to_all | solution.py:27
  172.2 2.8 copy.41
  175.0 2.4 reshape.131
  177.4 1.3 slice.9
  179.4 16.7 %collective-permute-done = bf16[4096,256]{1,0:T(8,128)(2,1)} collective-permute-done((bf16[4096,256]{1,0:T(8,128)(2,1)}, bf16[4096,256]{1,0:T(8,128)(2,1)}, u32[]{:S(2)}, u32[]{:S(2)}) %collective-permute-start) | collective-permute-done | bytes 2097184 | tf_op jit(solution)/shard_map/ppermute | solution.py:14
  196.1 2.2 slice.8
  198.4 2.3 copy.51
  200.7 4.3 %pad_maximum_fusion = (bf16[6144,2,128]{0,2,1:T(8,128)(2,1)}, bf16[6144,2,128]{0,2,1:T(8,128)(2,1)}) fusion(bf16[4096,2,128]{0,2,1:T(8,128)(2,1)S(1)} %copy-done.1, bf16[2048,2,128]{0,2,1:T(8,128)(2,1)} %bitcast.47, bf16[4096,2,128]{0,2,1:T(8,128)(2,1)} %concatenate.20, bf16[2048,2,128]{0,2,1:T(8,128)(2,1)S(1)} %bitcast.46), kind=kLoop, calls=%fused_computation.23 | loop fusion | flops 12582912 | bytes 12582912 | tf_op jit(solution)/shard_map/concatenate | solution.py:38
  205.0 132.3 %while.13 = (s32[]{:T(128)}, bf16[8,512,256]{2,1,0:T(8,128)(2,1)}, s32[8]{0:T(128)S(1)}, bf16[6144,2,128]{0,2,1:T(8,128)(2,1)}, s32[]{:T(128)}, /*index=5*/s32[4...) while((s32[]{:T(128)}, bf16[8,512,256]{2,1,0:T(8,128)(2,1)}, ...), condition=%wide.region_3.4_spmd, body=%wide.region_0.3_spmd.sunk | while | flops 1377830400 | bytes 40950536 | solution.py:74
  206.2 0.8 dynamic_slice.61
  207.0 2.0 compare_and_fusion.2
  209.0 3.9 fusion.36
  212.9 3.1 fusion.37
  216.0 4.6 %fusion.38 = bf16[512,2,128]{0,2,1:T(8,128)(2,1)S(1)} fusion(f32[2,512,2560]{2,1,0:T(8,128)S(1)} %get-tuple-element.238, f32[2,512]{1,0:T(2,128)S(1)} %get-tuple-element.239, pred[512,2560]{1,0:T(8,128)(4,1)S(1)} %compare_and_fusion.2, bf16[6144,2,128]{0,2,1:T(8,128)(2,1)} %get-tuple-element.271, s32[]{:T(128)S(6)} %select_n.49, ...), kind=kOutput, calls=%fused_computation.13.clone.1 | convolution fusion | flops 681836544 | bytes 13377540 | tf_op jit(solution)/shard_map/while/body/eval_jaxpr/hqk,khd->qhd/dot_general | solution.py:64
  222.8 0.8 dynamic_slice.61
  223.6 2.0 compare_and_fusion.2
  225.6 3.9 fusion.36
  229.4 3.1 fusion.37
  232.6 4.6 %fusion.38 = bf16[512,2,128]{0,2,1:T(8,128)(2,1)S(1)} fusion(f32[2,512,2560]{2,1,0:T(8,128)S(1)} %get-tuple-element.238, f32[2,512]{1,0:T(2,128)S(1)} %get-tuple-element.239, pred[512,2560]{1,0:T(8,128)(4,1)S(1)} %compare_and_fusion.2, bf16[6144,2,128]{0,2,1:T(8,128)(2,1)} %get-tuple-element.271, s32[]{:T(128)S(6)} %select_n.49, ...), kind=kOutput, calls=%fused_computation.13.clone.1 | convolution fusion | flops 681836544 | bytes 13377540 | tf_op jit(solution)/shard_map/while/body/eval_jaxpr/hqk,khd->qhd/dot_general | solution.py:64
  240.1 2.0 compare_and_fusion.2
  242.1 3.9 fusion.36
  246.0 3.1 fusion.37
  249.1 4.6 %fusion.38 = bf16[512,2,128]{0,2,1:T(8,128)(2,1)S(1)} fusion(f32[2,512,2560]{2,1,0:T(8,128)S(1)} %get-tuple-element.238, f32[2,512]{1,0:T(2,128)S(1)} %get-tuple-element.239, pred[512,2560]{1,0:T(8,128)(4,1)S(1)} %compare_and_fusion.2, bf16[6144,2,128]{0,2,1:T(8,128)(2,1)} %get-tuple-element.271, s32[]{:T(128)S(6)} %select_n.49, ...), kind=kOutput, calls=%fused_computation.13.clone.1 | convolution fusion | flops 681836544 | bytes 13377540 | tf_op jit(solution)/shard_map/while/body/eval_jaxpr/hqk,khd->qhd/dot_general | solution.py:64
  256.6 2.0 compare_and_fusion.2
  258.7 3.9 fusion.36
  262.5 3.1 fusion.37
  265.6 4.6 %fusion.38 = bf16[512,2,128]{0,2,1:T(8,128)(2,1)S(1)} fusion(f32[2,512,2560]{2,1,0:T(8,128)S(1)} %get-tuple-element.238, f32[2,512]{1,0:T(2,128)S(1)} %get-tuple-element.239, pred[512,2560]{1,0:T(8,128)(4,1)S(1)} %compare_and_fusion.2, bf16[6144,2,128]{0,2,1:T(8,128)(2,1)} %get-tuple-element.271, s32[]{:T(128)S(6)} %select_n.49, ...), kind=kOutput, calls=%fused_computation.13.clone.1 | convolution fusion | flops 681836544 | bytes 13377540 | tf_op jit(solution)/shard_map/while/body/eval_jaxpr/hqk,khd->qhd/dot_general | solution.py:64
  272.4 0.8 dynamic_slice.61
  273.2 2.0 compare_and_fusion.2
  275.2 3.9 fusion.36
  279.1 3.1 fusion.37
  282.2 4.6 %fusion.38 = bf16[512,2,128]{0,2,1:T(8,128)(2,1)S(1)} fusion(f32[2,512,2560]{2,1,0:T(8,128)S(1)} %get-tuple-element.238, f32[2,512]{1,0:T(2,128)S(1)} %get-tuple-element.239, pred[512,2560]{1,0:T(8,128)(4,1)S(1)} %compare_and_fusion.2, bf16[6144,2,128]{0,2,1:T(8,128)(2,1)} %get-tuple-element.271, s32[]{:T(128)S(6)} %select_n.49, ...), kind=kOutput, calls=%fused_computation.13.clone.1 | convolution fusion | flops 681836544 | bytes 13377540 | tf_op jit(solution)/shard_map/while/body/eval_jaxpr/hqk,khd->qhd/dot_general | solution.py:64
  289.7 2.0 compare_and_fusion.2
  291.7 3.9 fusion.36
  295.6 3.1 fusion.37
  298.7 4.6 %fusion.38 = bf16[512,2,128]{0,2,1:T(8,128)(2,1)S(1)} fusion(f32[2,512,2560]{2,1,0:T(8,128)S(1)} %get-tuple-element.238, f32[2,512]{1,0:T(2,128)S(1)} %get-tuple-element.239, pred[512,2560]{1,0:T(8,128)(4,1)S(1)} %compare_and_fusion.2, bf16[6144,2,128]{0,2,1:T(8,128)(2,1)} %get-tuple-element.271, s32[]{:T(128)S(6)} %select_n.49, ...), kind=kOutput, calls=%fused_computation.13.clone.1 | convolution fusion | flops 681836544 | bytes 13377540 | tf_op jit(solution)/shard_map/while/body/eval_jaxpr/hqk,khd->qhd/dot_general | solution.py:64
  305.5 0.8 dynamic_slice.61
  306.3 2.0 compare_and_fusion.2
  308.3 3.9 fusion.36
  312.1 3.1 fusion.37
  315.3 4.6 %fusion.38 = bf16[512,2,128]{0,2,1:T(8,128)(2,1)S(1)} fusion(f32[2,512,2560]{2,1,0:T(8,128)S(1)} %get-tuple-element.238, f32[2,512]{1,0:T(2,128)S(1)} %get-tuple-element.239, pred[512,2560]{1,0:T(8,128)(4,1)S(1)} %compare_and_fusion.2, bf16[6144,2,128]{0,2,1:T(8,128)(2,1)} %get-tuple-element.271, s32[]{:T(128)S(6)} %select_n.49, ...), kind=kOutput, calls=%fused_computation.13.clone.1 | convolution fusion | flops 681836544 | bytes 13377540 | tf_op jit(solution)/shard_map/while/body/eval_jaxpr/hqk,khd->qhd/dot_general | solution.py:64
  322.8 2.0 compare_and_fusion.2
  324.8 3.9 fusion.36
  328.7 3.1 fusion.37
  331.8 4.6 %fusion.38 = bf16[512,2,128]{0,2,1:T(8,128)(2,1)S(1)} fusion(f32[2,512,2560]{2,1,0:T(8,128)S(1)} %get-tuple-element.238, f32[2,512]{1,0:T(2,128)S(1)} %get-tuple-element.239, pred[512,2560]{1,0:T(8,128)(4,1)S(1)} %compare_and_fusion.2, bf16[6144,2,128]{0,2,1:T(8,128)(2,1)} %get-tuple-element.271, s32[]{:T(128)S(6)} %select_n.49, ...), kind=kOutput, calls=%fused_computation.13.clone.1 | convolution fusion | flops 681836544 | bytes 13377540 | tf_op jit(solution)/shard_map/while/body/eval_jaxpr/hqk,khd->qhd/dot_general | solution.py:64
  337.3 57.8 %all_to_all.73 = bf16[16,256,256]{2,1,0:T(8,128)(2,1)S(1)} all-to-all(bf16[16,256,256]{2,1,0:T(8,128)(2,1)} %bitcast.48), channel_id=1, replica_groups=mesh['blk'=16,'uly'=16] {'uly'}, dimensions={0} | all-to-all | bytes 4194304 | tf_op jit(solution)/shard_map/all_to_all | solution.py:76
  395.1 2.4 copy.49
  397.4 4.1 %copy.50 = bf16[256,4096]{1,0:T(8,128)(2,1)} copy(bf16[256,4096]{0,1:T(8,128)(2,1)} %bitcast.44) | data formatting | bytes 4194304 | tf_op jit(solution)/shard_map/all_to_all | solution.py:76
  (52 shorter events, 15.6 us)
Async XLA Ops:
  4.1 59.8 %all-to-all-start.2 = ((bf16[256,16,256]{0,2,1:T(8,128)(2,1)}), bf16[256,16,256]{0,2,1:T(8,128)(2,1)S(1)}, u32[]{:S(2)}, u32[]{:S(2)}) async-start(bf16[256,16,256]{0,2,1:T(8,128)(2,1)} %bitcast.42), calls=%async_computation.2 | async-start | bytes 4194304 | tf_op jit(solution)/shard_map/all_to_all | solution.py:28
  63.8 54.2 %all-to-all-start = ((bf16[256,16,256]{0,2,1:T(8,128)(2,1)}), bf16[256,16,256]{0,2,1:T(8,128)(2,1)}, u32[]{:S(2)}, u32[]{:S(2)}) async-start(bf16[256,16,256]{0,2,1:T(8,128)(2,1)} %bitcast.41), calls=%async_computation | async-start | bytes 4194304 | tf_op jit(solution)/shard_map/all_to_all | solution.py:29
  118.0 54.2 %all-to-all-start.1 = ((bf16[256,16,256]{0,2,1:T(8,128)(2,1)}), bf16[256,16,256]{0,2,1:T(8,128)(2,1)}, u32[]{:S(2)}, u32[]{:S(2)}) async-start(bf16[256,16,256]{0,2,1:T(8,128)(2,1)} %bitcast.40), calls=%async_computation.1 | async-start | bytes 4194304 | tf_op jit(solution)/shard_map/all_to_all | solution.py:27
  124.8 52.6 %collective-permute-start.1 = (bf16[4096,256]{1,0:T(8,128)(2,1)}, bf16[4096,256]{1,0:T(8,128)(2,1)}, u32[]{:S(2)}, u32[]{:S(2)}) collective-permute-start(bf16[4096,256]{1,0:T(8,128)(2,1)} %bitcast.50), channel_id=1, source_target_pairs={{0,16},{16,32},{32,48},{48,64},{64,80},{80,96},{96,112},{112,128},... | collective-permute-start | bytes 6291464 | tf_op jit(solution)/shard_map/ppermute | solution.py:14
  130.7 65.5 %collective-permute-start = (bf16[4096,256]{1,0:T(8,128)(2,1)}, bf16[4096,256]{1,0:T(8,128)(2,1)}, u32[]{:S(2)}, u32[]{:S(2)}) collective-permute-start(bf16[4096,256]{1,0:T(8,128)(2,1)} %bitcast.49), channel_id=1, source_target_pairs={{0,16},{16,32},{32,48},{48,64},{64,80},{80,96},{96,112},{112,128},... | collective-permute-start | bytes 6291464 | tf_op jit(solution)/shard_map/ppermute | solution.py:14
  141.1 4.3 %copy-start = (bf16[16,256,256]{1,0,2:T(8,128)(2,1)S(1)}, bf16[16,256,256]{1,0,2:T(8,128)(2,1)}, u32[]{:S(2)}) copy-start(bf16[16,256,256]{1,0,2:T(8,128)(2,1)} %copy.45) | copy-start | bytes 6291460
  179.4 21.3 %copy-start.1 = (bf16[4096,2,128]{0,2,1:T(8,128)(2,1)S(1)}, bf16[4096,2,128]{0,2,1:T(8,128)(2,1)}, u32[]{:S(2)}) copy-start(bf16[4096,2,128]{0,2,1:T(8,128)(2,1)} %concatenate.17) | copy-start | bytes 6291460
where the time goes:
time: 403 us; the launch traced here: 401 us
  waiting for transfers between devices  133 us (33%)
  local copies, waits for them, and re-layouts  67.8 us (17%)
  matrix products  67.8 us (17%)
  blocking collectives  57.8 us (14%)
  other arithmetic  45.4 us (11%)
  starting transfers between devices  23.8 us (6%)
  loops' own time  5.49 us (1%)
    all_to_all x1, blocking collectives, shards(): lax.all_to_all(result, 'uly', split_axis=0, concat_axis=1, tiled=True)  57.8 us
    all_to_all x1, waiting for transfers between devices, shards(): lax.all_to_all(keys, 'uly', split_axis=1, concat_axis=0, tiled=True)  46.5 us
    all_to_all x1, waiting for transfers between devices, shards(): lax.all_to_all(values, 'uly', split_axis=1, concat_axis=0, tiled=True)  45.6 us
    dot_general x8, matrix products, attend_span(): jnp.einsum('hqk,khd->qhd', weights, value_rows, preferred_element_type=jn...  37 us
    dot_general x8, matrix products, attend_span(): jnp.einsum('qhd,khd->hqk', query_rows, key_rows, preferred_element_type=j...  30.8 us
    reduce_sum x8, other arithmetic, attend_span(): totals = jnp.sum(probs, axis=-1)  25 us
    all_to_all x1, waiting for transfers between devices, shards(): lax.all_to_all(queries, 'uly', split_axis=1, concat_axis=0, tiled=True)  24.5 us
    ppermute x2, waiting for transfers between devices, shifted(): return lax.ppermute(block, axis, route)  16.7 us
  transfers between devices with their start and end apart: 5, of which 4 were waited for; matrix products, arithmetic and copies ran while one was open for 9% of the time, Pallas kernels for 0%

commit v1 on v0

v1 whole, which is shorter than its diff:
```python
import functools
import math

import jax
import jax.numpy as jnp
from jax import lax
from jax.experimental import pallas as pl
from jax.experimental.pallas import tpu as pltpu
from jax.sharding import PartitionSpec as P

HEAD_DIM = 128
LANES = 128
MESH = pl.DeviceIdType.MESH
LAST_DIMS = (((1,), (1,)), ((), ()))
SCALE = math.log2(math.e) / math.sqrt(HEAD_DIM)
Q, K, V = 0, 1, 2


def kernel(
    peers, stretches, rows, heads,
    queries, keys, values, doc_start, attended,
    q_buf, k_buf, v_buf, o_buf, oldest, scores,
    in_send, in_recv, halo_send, halo_recv, out_send, out_recv,
):
    stretch = peers * rows
    window = stretch // 2
    span = window + rows
    blk, me = lax.axis_index("blk"), lax.axis_index("uly")
    after, before = lax.rem(blk + 1, stretches), lax.rem(blk + stretches - 1, stretches)

    def peer(i):
        half = (i + 1) // 2
        return lax.rem(me + jnp.where(i % 2 == 1, half, peers - half), peers)

    def token_rows(p, shift=0):
        return pl.ds(pl.multiple_of(p * rows + shift, rows), rows)

    def head_columns(p, head):
        return pl.ds(pl.multiple_of((p * heads + head) * HEAD_DIM, HEAD_DIM), HEAD_DIM)

    barrier = pltpu.get_barrier_semaphore()

    def greet(i, carry):
        pl.semaphore_signal(barrier, inc=1, device_id=(blk, peer(i)), device_id_type=MESH)
        return carry

    lax.fori_loop(1, peers, greet, 0)
    pl.semaphore_signal(barrier, inc=1, device_id=(before, me), device_id_type=MESH)
    pl.semaphore_wait(barrier, peers)

    operands = {Q: (queries, q_buf, 0), K: (keys, k_buf, window), V: (values, v_buf, window)}
    order = (K, V, Q)

    def inbound(head, t, src_peer, dst_peer):
        source, buffer, shift = operands[t]
        return pltpu.make_async_remote_copy(
            src_ref=source.at[:, head_columns(dst_peer, head)],
            dst_ref=buffer.at[head, token_rows(src_peer, shift)],
            send_sem=in_send.at[head, t, dst_peer],
            recv_sem=in_recv.at[head, t, src_peer],
            device_id=(blk, dst_peer),
            device_id_type=MESH,
        )

    def own(head, t):
        source, buffer, shift = operands[t]
        return pltpu.make_async_copy(
            source.at[:, head_columns(me, head)],
            buffer.at[head, token_rows(me, shift)],
            in_recv.at[head, t, me],
        )

    for head in range(heads):
        for t in order:
            own(head, t).start()

            def send(i, carry):
                p = peer(i)
                inbound(head, t, me, p).start()
                return carry

            lax.fori_loop(1, peers, send, 0)

    for group in range(stretch // LANES):
        starts = jnp.transpose(jnp.broadcast_to(doc_start[group : group + 1, :], (LANES, LANES)))
        token = group * LANES + lax.broadcasted_iota(jnp.int32, (LANES, LANES), 0)
        oldest[group * LANES : (group + 1) * LANES, :] = jnp.maximum(
            starts - blk * stretch + window, token + 1
        )

    def arrived(head, t, low, high):
        def wait(p, carry):
            inbound(head, t, p, me).wait_recv()
            return carry

        lax.fori_loop(low, high, wait, 0)

    def halo(head, t):
        buffer = operands[t][1]
        return pltpu.make_async_remote_copy(
            src_ref=buffer.at[head, pl.ds(stretch, window)],
            dst_ref=buffer.at[head, pl.ds(0, window)],
            send_sem=halo_send.at[head, t],
            recv_sem=halo_recv.at[head, t],
            device_id=(after, me),
            device_id_type=MESH,
        )

    def outbound(head, src_peer, dst_peer):
        return pltpu.make_async_remote_copy(
            src_ref=o_buf.at[head, token_rows(dst_peer)],
            dst_ref=attended.at[:, head_columns(src_peer, head)],
            send_sem=out_send.at[head, dst_peer],
            recv_sem=out_recv.at[head, src_peer],
            device_id=(blk, dst_peer),
            device_id_type=MESH,
        )

    def own_out(head):
        return pltpu.make_async_copy(
            o_buf.at[head, token_rows(me)],
            attended.at[:, head_columns(me, head)],
            out_recv.at[head, me],
        )

    def send_out(head, p):
        @pl.when(p == me)
        def _():
            own_out(head).start()

        @pl.when(p != me)
        def _():
            outbound(head, me, p).start()

    def attend(head, p):
        first = p * rows

        def key_rows(c):
            return pl.ds(pl.multiple_of(first + c * rows, rows), rows)

        query = q_buf[head, token_rows(p)]
        low = oldest[token_rows(p)] - first
        lane = lax.broadcasted_iota(jnp.int32, (rows, LANES), 1)
        row = lax.broadcasted_iota(jnp.int32, (rows, LANES), 0)
        top = jnp.full((rows, LANES), -jnp.inf, jnp.float32)
        for c in range(span // rows):
            tile = lax.dot_general(
                query, k_buf[head, key_rows(c)], LAST_DIMS, preferred_element_type=jnp.float32
            )
            for at in range(c * rows, (c + 1) * rows, LANES):
                allowed = lane + at >= low
                if at >= window:
                    allowed = allowed & (lane <= row - (at - window))
                part = jnp.where(allowed, tile[:, at - c * rows : at - c * rows + LANES], -jnp.inf)
                top = jnp.maximum(top, part)
                scores[:, at : at + LANES] = part
        row_max = jnp.broadcast_to(jnp.max(top, axis=1, keepdims=True) * SCALE, (rows, LANES))
        mixed = jnp.zeros((rows, HEAD_DIM), jnp.float32)
        total = jnp.zeros((rows, LANES), jnp.float32)
        for c in range(span // rows):
            weights = []
            for at in range(c * rows, (c + 1) * rows, LANES):
                probs = jnp.exp2(scores[:, at : at + LANES] * SCALE - row_max)
                total = total + probs
                weights.append(probs.astype(jnp.bfloat16))
            mixed = mixed + jnp.dot(
                jnp.concatenate(weights, axis=1),
                v_buf[head, key_rows(c)],
                preferred_element_type=jnp.float32,
            )
        mixed = mixed / jnp.sum(total, axis=1, keepdims=True)
        o_buf[head, token_rows(p)] = mixed.astype(jnp.bfloat16)

    middle = peers // 2
    for head in range(heads):
        for t in (K, V):
            arrived(head, t, middle, peers)
            halo(head, t).start()
        for t in (K, V):
            arrived(head, t, 0, middle)
        arrived(head, Q, 0, peers)

        def block(p, carry):
            attend(head, p)
            send_out(head, p)
            return carry

        lax.fori_loop(middle, peers, block, 0)
        for t in (K, V):
            halo(head, t).wait_recv()
        lax.fori_loop(0, middle, block, 0)

    for head in range(heads):
        for t in (K, V):
            halo(head, t).wait_send()

        def settle(i, carry):
            p = peer(i)
            for t in order:
                inbound(head, t, me, p).wait_send()
            outbound(head, p, p).wait_recv()
            outbound(head, me, p).wait_send()
            return carry

        lax.fori_loop(1, peers, settle, 0)
        own_out(head).wait()


def shards(peers, stretches, queries, keys, values, doc_start):
    rows, width = queries.shape
    stretch = rows * peers
    window = stretch // 2
    heads = width // peers // HEAD_DIM
    anywhere = pl.BlockSpec(memory_space=pl.ANY)
    return pl.pallas_call(
        functools.partial(kernel, peers, stretches, rows, heads),
        out_shape=jax.ShapeDtypeStruct((rows, width), jnp.bfloat16),
        in_specs=[anywhere, anywhere, anywhere, pl.BlockSpec(memory_space=pltpu.VMEM)],
        out_specs=anywhere,
        scratch_shapes=[
            pltpu.VMEM((heads, stretch, HEAD_DIM), jnp.bfloat16),
            pltpu.VMEM((heads, stretch + window, HEAD_DIM), jnp.bfloat16),
            pltpu.VMEM((heads, stretch + window, HEAD_DIM), jnp.bfloat16),
            pltpu.VMEM((heads, stretch, HEAD_DIM), jnp.bfloat16),
            pltpu.VMEM((stretch, LANES), jnp.int32),
            pltpu.VMEM((rows, window + rows), jnp.float32),
            pltpu.SemaphoreType.DMA((heads, 3, peers)),
            pltpu.SemaphoreType.DMA((heads, 3, peers)),
            pltpu.SemaphoreType.DMA((heads, 3)),
            pltpu.SemaphoreType.DMA((heads, 3)),
            pltpu.SemaphoreType.DMA((heads, peers)),
            pltpu.SemaphoreType.DMA((heads, peers)),
        ],
        compiler_params=pltpu.CompilerParams(
            collective_id=0, has_side_effects=True, vmem_limit_bytes=48 << 20
        ),
    )(queries, keys, values, doc_start.reshape(stretch // LANES, LANES))


def solution(mesh):
    rows = P(("blk", "uly"), None)
    return jax.shard_map(
        functools.partial(shards, mesh.shape["uly"], mesh.shape["blk"]),
        mesh=mesh,
        in_specs=(rows, rows, rows, P("blk")),
        out_specs=rows,
        check_vma=False,
    )
```

time: 403 us -> 196 us (0.49)
  the two profiles are of different devices: /device:TPU:12 before, /device:TPU:91 now
where the time goes in v1:
time: 196 us
  Pallas kernels  192 us (98%)
  local copies, waits for them, and re-layouts  3.63 us (2%)
    pallas_call x1, Pallas kernels, shards(): pl.pallas_call(functools.partial(kernel, peers, stretches, rows, heads),...  192 us

profile of v1, /device:TPU:91, one launch (start us, length us, event | category | flops | bytes accessed | tf_op | source)
XLA Modules:
  0.0 195.9 jit_solution(4523016871718502208)
XLA Ops:
  0.0 0.0 copy-start
  0.0 1.6 copy-done
  1.6 0.0 copy-start.1
  1.6 0.7 copy-done.1
  2.3 192.3 %shard_map.46 = bf16[256,4096]{1,0:T(8,128)(2,1)S(1)} custom-call(bf16[256,4096]{1,0:T(8,128)(2,1)S(1)} %copy-done, bf16[256,4096]{1,0:T(8,128)(2,1)} %keys.1, bf16[256,4096]{1,0:T(8,128)(2,1)} %values.1, s32[32,128]{1,0:T(8,128)S(1)} %bitcast.1), custom_call_target="tpu_custom_call" | custom-call | tf_op jit(solution)/shard_map/pallas_call | solution.py:215
  194.6 1.3 copy.6
Async XLA Ops:
  0.0 1.6 copy-start
  1.6 0.7 copy-start.1

commit v2 on v1

--- a/solution.py
+++ b/solution.py
@@ -19,7 +19,7 @@
 def kernel(
     peers, stretches, rows, heads,
     queries, keys, values, doc_start, attended,
-    q_buf, k_buf, v_buf, o_buf, oldest, scores,
+    q_buf, k_buf, v_buf, o_buf, doc_buf, oldest, scores, doc_sem,
     in_send, in_recv, halo_send, halo_recv, out_send, out_recv,
 ):
     stretch = peers * rows
@@ -38,6 +38,8 @@
     def head_columns(p, head):
         return pl.ds(pl.multiple_of((p * heads + head) * HEAD_DIM, HEAD_DIM), HEAD_DIM)
 
+    fetch = pltpu.make_async_copy(doc_start, doc_buf, doc_sem)
+    fetch.start()
     barrier = pltpu.get_barrier_semaphore()
 
     def greet(i, carry):
@@ -81,8 +83,9 @@
 
             lax.fori_loop(1, peers, send, 0)
 
+    fetch.wait()
     for group in range(stretch // LANES):
-        starts = jnp.transpose(jnp.broadcast_to(doc_start[group : group + 1, :], (LANES, LANES)))
+        starts = jnp.transpose(jnp.broadcast_to(doc_buf[group : group + 1, :], (LANES, LANES)))
         token = group * LANES + lax.broadcasted_iota(jnp.int32, (LANES, LANES), 0)
         oldest[group * LANES : (group + 1) * LANES, :] = jnp.maximum(
             starts - blk * stretch + window, token + 1
@@ -215,15 +218,17 @@
     return pl.pallas_call(
         functools.partial(kernel, peers, stretches, rows, heads),
         out_shape=jax.ShapeDtypeStruct((rows, width), jnp.bfloat16),
-        in_specs=[anywhere, anywhere, anywhere, pl.BlockSpec(memory_space=pltpu.VMEM)],
+        in_specs=[pl.BlockSpec(memory_space=pltpu.HBM)] * 4,
         out_specs=anywhere,
         scratch_shapes=[
             pltpu.VMEM((heads, stretch, HEAD_DIM), jnp.bfloat16),
             pltpu.VMEM((heads, stretch + window, HEAD_DIM), jnp.bfloat16),
             pltpu.VMEM((heads, stretch + window, HEAD_DIM), jnp.bfloat16),
             pltpu.VMEM((heads, stretch, HEAD_DIM), jnp.bfloat16),
+            pltpu.VMEM((stretch // LANES, LANES), jnp.int32),
             pltpu.VMEM((stretch, LANES), jnp.int32),
             pltpu.VMEM((rows, window + rows), jnp.float32),
+            pltpu.SemaphoreType.DMA,
             pltpu.SemaphoreType.DMA((heads, 3, peers)),
             pltpu.SemaphoreType.DMA((heads, 3, peers)),
             pltpu.SemaphoreType.DMA((heads, 3)),
@@ -234,7 +239,7 @@
         compiler_params=pltpu.CompilerParams(
             collective_id=0, has_side_effects=True, vmem_limit_bytes=48 << 20
         ),
-    )(queries, keys, values, doc_start.reshape(stretch // LANES, LANES))
+    )(*(pltpu.with_memory_space_constraint(a, pltpu.HBM) for a in (queries, keys, values, doc_start.reshape(stretch // LANES, LANES))))
 
 
 def solution(mesh):

time: 196 us -> 194 us (0.990)
  local copies, waits for them, and re-layouts: 3.63 us -> 1.32 us
    unnamed x5 -> x1, local copies, waits for them, and re-layouts: 3.63 us -> 1.32 us
where the time goes in v2:
time: 194 us; the launch traced here: 193 us
  Pallas kernels  192 us (99%)
    pallas_call x1, Pallas kernels, shards(): pl.pallas_call(functools.partial(kernel, peers, stretches, rows, heads),...  192 us

profile of v2, /device:TPU:91, one launch (start us, length us, event | category | flops | bytes accessed | tf_op | source)
XLA Modules:
  0.0 193.4 jit_solution(8225663431472405293)
XLA Ops:
  0.0 192.1 %shard_map.46 = bf16[256,4096]{1,0:T(8,128)(2,1)S(1)} custom-call(bf16[256,4096]{1,0:T(8,128)(2,1)} %queries.1, bf16[256,4096]{1,0:T(8,128)(2,1)} %keys.1, bf16[256,4096]{1,0:T(8,128)(2,1)} %values.1, s32[32,128]{1,0:T(8,128)} %bitcast.1), custom_call_target="tpu_custom_call" | custom-call | tf_op jit(solution)/shard_map/pallas_call | solution.py:218
  192.1 1.3 copy.6

commit v3 on v2

--- a/solution.py
+++ b/solution.py
@@ -23,6 +23,7 @@
     in_send, in_recv, halo_send, halo_recv, out_send, out_recv,
 ):
     stretch = peers * rows
+    middle = peers // 2
     window = stretch // 2
     span = window + rows
     blk, me = lax.axis_index("blk"), lax.axis_index("uly")
@@ -32,6 +33,9 @@
         half = (i + 1) // 2
         return lax.rem(me + jnp.where(i % 2 == 1, half, peers - half), peers)
 
+    def served(i):
+        return jnp.where(i < middle, i, peers - 1 - i + middle)
+
     def token_rows(p, shift=0):
         return pl.ds(pl.multiple_of(p * rows + shift, rows), rows)
 
@@ -40,6 +44,7 @@
 
     fetch = pltpu.make_async_copy(doc_start, doc_buf, doc_sem)
     fetch.start()
+
     barrier = pltpu.get_barrier_semaphore()
 
     def greet(i, carry):
@@ -174,24 +179,23 @@
         mixed = mixed / jnp.sum(total, axis=1, keepdims=True)
         o_buf[head, token_rows(p)] = mixed.astype(jnp.bfloat16)
 
-    middle = peers // 2
     for head in range(heads):
         for t in (K, V):
             arrived(head, t, middle, peers)
             halo(head, t).start()
         for t in (K, V):
             arrived(head, t, 0, middle)
-        arrived(head, Q, 0, peers)
-
-        def block(p, carry):
+        for t in (K, V):
+            halo(head, t).wait_recv()
+
+        def block(i, carry):
+            p = served(i)
+            inbound(head, Q, p, me).wait_recv()
             attend(head, p)
             send_out(head, p)
             return carry
 
-        lax.fori_loop(middle, peers, block, 0)
-        for t in (K, V):
-            halo(head, t).wait_recv()
-        lax.fori_loop(0, middle, block, 0)
+        lax.fori_loop(0, peers, block, 0)
 
     for head in range(heads):
         for t in (K, V):
@@ -214,12 +218,12 @@
     stretch = rows * peers
     window = stretch // 2
     heads = width // peers // HEAD_DIM
-    anywhere = pl.BlockSpec(memory_space=pl.ANY)
+    operands = (queries, keys, values, doc_start.reshape(stretch // LANES, LANES))
     return pl.pallas_call(
         functools.partial(kernel, peers, stretches, rows, heads),
         out_shape=jax.ShapeDtypeStruct((rows, width), jnp.bfloat16),
         in_specs=[pl.BlockSpec(memory_space=pltpu.HBM)] * 4,
-        out_specs=anywhere,
+        out_specs=pl.BlockSpec(memory_space=pl.ANY),
         scratch_shapes=[
             pltpu.VMEM((heads, stretch, HEAD_DIM), jnp.bfloat16),
             pltpu.VMEM((heads, stretch + window, HEAD_DIM), jnp.bfloat16),
@@ -239,7 +243,7 @@
         compiler_params=pltpu.CompilerParams(
             collective_id=0, has_side_effects=True, vmem_limit_bytes=48 << 20
         ),
-    )(*(pltpu.with_memory_space_constraint(a, pltpu.HBM) for a in (queries, keys, values, doc_start.reshape(stretch // LANES, LANES))))
+    )(*(pltpu.with_memory_space_constraint(operand, pltpu.HBM) for operand in operands))
 
 
 def solution(mesh):

time: 194 us -> 193 us (level)
  no operation moved by 1% of the time
where the time goes in v3:
time: 193 us
  Pallas kernels  192 us (99%)
    pallas_call x1, Pallas kernels, shards(): pl.pallas_call(functools.partial(kernel, peers, stretches, rows, heads),...  192 us

profile of v3, /device:TPU:91, one launch (start us, length us, event | category | flops | bytes accessed | tf_op | source)
XLA Modules:
  0.0 192.8 jit_solution(2304965680007669579)
XLA Ops:
  0.0 191.5 %shard_map.46 = bf16[256,4096]{1,0:T(8,128)(2,1)S(1)} custom-call(bf16[256,4096]{1,0:T(8,128)(2,1)} %queries.1, bf16[256,4096]{1,0:T(8,128)(2,1)} %keys.1, bf16[256,4096]{1,0:T(8,128)(2,1)} %values.1, s32[32,128]{1,0:T(8,128)} %bitcast.1), custom_call_target="tpu_custom_call" | custom-call | tf_op jit(solution)/shard_map/pallas_call | solution.py:222
  191.5 1.3 copy.6

commit v4 on v3

--- a/solution.py
+++ b/solution.py
@@ -20,7 +20,7 @@
     peers, stretches, rows, heads,
     queries, keys, values, doc_start, attended,
     q_buf, k_buf, v_buf, o_buf, doc_buf, oldest, scores, doc_sem,
-    in_send, in_recv, halo_send, halo_recv, out_send, out_recv,
+    in_send, in_recv, halo_send, halo_recv, out_send, out_recv, out_own,
 ):
     stretch = peers * rows
     middle = peers // 2
@@ -63,7 +63,7 @@
         return pltpu.make_async_remote_copy(
             src_ref=source.at[:, head_columns(dst_peer, head)],
             dst_ref=buffer.at[head, token_rows(src_peer, shift)],
-            send_sem=in_send.at[head, t, dst_peer],
+            send_sem=in_send.at[t],
             recv_sem=in_recv.at[head, t, src_peer],
             device_id=(blk, dst_peer),
             device_id_type=MESH,
@@ -118,8 +118,8 @@
         return pltpu.make_async_remote_copy(
             src_ref=o_buf.at[head, token_rows(dst_peer)],
             dst_ref=attended.at[:, head_columns(src_peer, head)],
-            send_sem=out_send.at[head, dst_peer],
-            recv_sem=out_recv.at[head, src_peer],
+            send_sem=out_send,
+            recv_sem=out_recv,
             device_id=(blk, dst_peer),
             device_id_type=MESH,
         )
@@ -128,7 +128,7 @@
         return pltpu.make_async_copy(
             o_buf.at[head, token_rows(me)],
             attended.at[:, head_columns(me, head)],
-            out_recv.at[head, me],
+            out_own.at[head],
         )
 
     def send_out(head, p):
@@ -197,20 +197,25 @@
 
         lax.fori_loop(0, peers, block, 0)
 
+    def remote_columns(send_sem):
+        columns = pl.ds(0, (peers - 1) * heads * HEAD_DIM)
+        return pltpu.make_async_remote_copy(
+            src_ref=queries.at[:, columns],
+            dst_ref=attended.at[:, columns],
+            send_sem=send_sem,
+            recv_sem=out_recv,
+            device_id=(after, me),
+            device_id_type=MESH,
+        )
+
     for head in range(heads):
         for t in (K, V):
             halo(head, t).wait_send()
-
-        def settle(i, carry):
-            p = peer(i)
-            for t in order:
-                inbound(head, t, me, p).wait_send()
-            outbound(head, p, p).wait_recv()
-            outbound(head, me, p).wait_send()
-            return carry
-
-        lax.fori_loop(1, peers, settle, 0)
         own_out(head).wait()
+    for t in order:
+        remote_columns(in_send.at[t]).wait_send()
+    remote_columns(out_send).wait_send()
+    remote_columns(out_send).wait_recv()
 
 
 def shards(peers, stretches, queries, keys, values, doc_start):
@@ -233,12 +238,13 @@
             pltpu.VMEM((stretch, LANES), jnp.int32),
             pltpu.VMEM((rows, window + rows), jnp.float32),
             pltpu.SemaphoreType.DMA,
-            pltpu.SemaphoreType.DMA((heads, 3, peers)),
+            pltpu.SemaphoreType.DMA((3,)),
             pltpu.SemaphoreType.DMA((heads, 3, peers)),
             pltpu.SemaphoreType.DMA((heads, 3)),
             pltpu.SemaphoreType.DMA((heads, 3)),
-            pltpu.SemaphoreType.DMA((heads, peers)),
-            pltpu.SemaphoreType.DMA((heads, peers)),
+            pltpu.SemaphoreType.DMA,
+            pltpu.SemaphoreType.DMA,
+            pltpu.SemaphoreType.DMA((heads,)),
         ],
         compiler_params=pltpu.CompilerParams(
             collective_id=0, has_side_effects=True, vmem_limit_bytes=48 << 20

time: 193 us -> 192 us (level)
  Pallas kernels: 192 us -> 190 us
where the time goes in v4:
time: 192 us; the launch traced here: 191 us
  Pallas kernels  190 us (99%)
    pallas_call x1, Pallas kernels, shards(): pl.pallas_call(functools.partial(kernel, peers, stretches, rows, heads),...  190 us

profile of v4, /device:TPU:91, one launch (start us, length us, event | category | flops | bytes accessed | tf_op | source)
XLA Modules:
  0.0 191.5 jit_solution(10316431484921112974)
XLA Ops:
  0.0 190.1 %shard_map.46 = bf16[256,4096]{1,0:T(8,128)(2,1)S(1)} custom-call(bf16[256,4096]{1,0:T(8,128)(2,1)} %queries.1, bf16[256,4096]{1,0:T(8,128)(2,1)} %keys.1, bf16[256,4096]{1,0:T(8,128)(2,1)} %values.1, s32[32,128]{1,0:T(8,128)} %bitcast.1), custom_call_target="tpu_custom_call" | custom-call | tf_op jit(solution)/shard_map/pallas_call | solution.py:227
  190.1 1.3 copy.6

commit v5 on v4

--- a/solution.py
+++ b/solution.py
@@ -34,16 +34,14 @@
         return lax.rem(me + jnp.where(i % 2 == 1, half, peers - half), peers)
 
     def served(i):
-        return jnp.where(i < middle, i, peers - 1 - i + middle)
+        places = sum(jnp.where(i // 2 == k, 2 * z, 0) for k, z in enumerate((0, 1, 2, 3, 6, 7, 5, 4)))
+        return places + i % 2
 
     def token_rows(p, shift=0):
         return pl.ds(pl.multiple_of(p * rows + shift, rows), rows)
 
     def head_columns(p, head):
         return pl.ds(pl.multiple_of((p * heads + head) * HEAD_DIM, HEAD_DIM), HEAD_DIM)
-
-    fetch = pltpu.make_async_copy(doc_start, doc_buf, doc_sem)
-    fetch.start()
 
     barrier = pltpu.get_barrier_semaphore()
 
@@ -79,7 +77,6 @@
 
     for head in range(heads):
         for t in order:
-            own(head, t).start()
 
             def send(i, carry):
                 p = peer(i)
@@ -87,7 +84,10 @@
                 return carry
 
             lax.fori_loop(1, peers, send, 0)
-
+            own(head, t).start()
+
+    fetch = pltpu.make_async_copy(doc_start, doc_buf, doc_sem)
+    fetch.start()
     fetch.wait()
     for group in range(stretch // LANES):
         starts = jnp.transpose(jnp.broadcast_to(doc_buf[group : group + 1, :], (LANES, LANES)))

time: 192 us -> 192 us (level)
  no operation moved by 1% of the time
where the time goes in v5:
time: 192 us; the launch traced here: 191 us
  Pallas kernels  190 us (99%)
    pallas_call x1, Pallas kernels, shards(): pl.pallas_call(functools.partial(kernel, peers, stretches, rows, heads),...  190 us

profile of v5, /device:TPU:91, one launch (start us, length us, event | category | flops | bytes accessed | tf_op | source)
XLA Modules:
  0.0 191.4 jit_solution(15839432470937953606)
XLA Ops:
  0.0 190.1 %shard_map.46 = bf16[256,4096]{1,0:T(8,128)(2,1)S(1)} custom-call(bf16[256,4096]{1,0:T(8,128)(2,1)} %queries.1, bf16[256,4096]{1,0:T(8,128)(2,1)} %keys.1, bf16[256,4096]{1,0:T(8,128)(2,1)} %values.1, s32[32,128]{1,0:T(8,128)} %bitcast.1), custom_call_target="tpu_custom_call" | custom-call | tf_op jit(solution)/shard_map/pallas_call | solution.py:227
  190.1 1.3 copy.6

commit v6 on v4

--- a/solution.py
+++ b/solution.py
@@ -34,7 +34,8 @@
         return lax.rem(me + jnp.where(i % 2 == 1, half, peers - half), peers)
 
     def served(i):
-        return jnp.where(i < middle, i, peers - 1 - i + middle)
+        places = sum(jnp.where(i // 2 == k, 2 * z, 0) for k, z in enumerate((0, 1, 2, 3, 6, 7, 5, 4)))
+        return places + i % 2
 
     def token_rows(p, shift=0):
         return pl.ds(pl.multiple_of(p * rows + shift, rows), rows)

time: 192 us -> 192 us (level)
  no operation moved by 1% of the time
where the time goes in v6:
time: 192 us; the launch traced here: 191 us
  Pallas kernels  190 us (99%)
    pallas_call x1, Pallas kernels, shards(): pl.pallas_call(functools.partial(kernel, peers, stretches, rows, heads),...  190 us

profile of v6, /device:TPU:91, one launch (start us, length us, event | category | flops | bytes accessed | tf_op | source)
XLA Modules:
  0.0 191.5 jit_solution(16220597660399578942)
XLA Ops:
  0.0 190.1 %shard_map.46 = bf16[256,4096]{1,0:T(8,128)(2,1)S(1)} custom-call(bf16[256,4096]{1,0:T(8,128)(2,1)} %queries.1, bf16[256,4096]{1,0:T(8,128)(2,1)} %keys.1, bf16[256,4096]{1,0:T(8,128)(2,1)} %values.1, s32[32,128]{1,0:T(8,128)} %bitcast.1), custom_call_target="tpu_custom_call" | custom-call | tf_op jit(solution)/shard_map/pallas_call | solution.py:228
  190.1 1.3 copy.6
